TPU v7x, 512 devices: a whole 4x4x16 slice. The times are simulated.
512 devices in a mesh: dp: 64 (over y_hi, z, core), seq: 8 (over x, y_lo).
Axes of the slice: x: 4, y: 4 (y_hi: 2, y_lo: 2; y = y_hi * 2 + y_lo), z: 16, core: 2. Of those that a mesh axis runs over, the one named last changes fastest.
Arguments:
- queries: bfloat16 [65536, 4096], P(('dp', 'seq')), may hold values from -180 to 180, as said below
- keys: bfloat16 [65536, 512], P(('dp', 'seq')), may hold values from -6 to 6, as said below
- values: bfloat16 [65536, 512], P(('dp', 'seq')), may hold values from -6 to 6
- lengths: int32 [64, 16], P('dp'), may hold values from 1 to 512, 1024 in all within a row
- out_grad: bfloat16 [65536, 4096], P(('dp', 'seq')), may hold values from -6 to 6
Outputs:
- attended: bfloat16 [65536, 4096], P(('dp', 'seq'))
- query_grad: bfloat16 [65536, 4096], P(('dp', 'seq'))
- key_grad: bfloat16 [65536, 512], P(('dp', 'seq'))
- value_grad: bfloat16 [65536, 512], P(('dp', 'seq'))
Inputs may be any that keep to these rules, and one draw needn't show every extreme that they name: `queries`: queries stay within this range. `keys`: keys stay within this range.
All inputs are finite; a program needn't handle non-finite values.
Results may differ from a plain program's by a relative error of at most 0.0095.
Values may be sent and summed in bfloat16 or wider, within the bound.
No kernel may reach another device: no remote copies, remote signals or barrier semaphores. Data moves between devices by JAX's collectives and lax.ppermute only.
A program may use at most 64 MiB of HBM per device.

v0:
```python
import jax
import jax.numpy as jnp
from jax import lax
from jax.sharding import PartitionSpec as P

H = 32
KVH = 4
HD = 128
GROUP = 8


def doc_of(pos, ends):
    return jnp.sum((pos[:, None] >= ends[None, :]).astype(jnp.int32), axis=1)


def shards(queries, keys, values, lengths, out_grad):
    tok_rows = queries.shape[0]
    kv_width = keys.shape[1]
    scale = HD ** (-0.5)
    qh = queries.reshape(tok_rows, KVH, GROUP, HD)
    grad_heads = out_grad.reshape(tok_rows, KVH, GROUP, HD)
    ends = jnp.cumsum(lengths[0])
    seq_pos = lax.axis_index("seq") * tok_rows + jnp.arange(tok_rows, dtype=jnp.int32)
    query_doc = doc_of(seq_pos, ends)
    total_len = tok_rows * lax.axis_size("seq")
    block = min(512, total_len)
    live_blocks = seq_pos[-1] // block + 1

    def visible_of(kstart, count):
        kpos = kstart + jnp.arange(count, dtype=jnp.int32)
        return (doc_of(kpos, ends)[None, :] == query_doc[:, None]) & (
            kpos[None, :] <= seq_pos[:, None]
        )

    def scores_of(key_rows, visible):
        raw = (
            jnp.einsum(
                "tkgd,skd->kgts",
                qh,
                key_rows.reshape(-1, KVH, HD),
                preferred_element_type=jnp.float32,
            )
            * scale
        )
        return jnp.where(visible, raw, -1e30)

    def forward_step(carry, key_rows, value_rows, kstart):
        top, lsum, acc = carry
        visible = visible_of(kstart, key_rows.shape[0])
        scores = scores_of(key_rows, visible)
        top_new = jnp.maximum(top, jnp.max(scores, axis=-1))
        rescale = jnp.exp(top - top_new)
        expo = jnp.where(visible, jnp.exp(scores - top_new[..., None]), 0.0)
        lsum = lsum * rescale + jnp.sum(expo, axis=-1)
        acc = acc * rescale[..., None] + jnp.einsum(
            "kgts,skd->kgtd",
            expo.astype(jnp.bfloat16),
            value_rows.reshape(-1, KVH, HD),
            preferred_element_type=jnp.float32,
        )
        return (top_new, lsum, acc)

    start_carry = (
        jnp.full((KVH, GROUP, tok_rows), -1e30, jnp.float32),
        jnp.zeros((KVH, GROUP, tok_rows), jnp.float32),
        jnp.zeros((KVH, GROUP, tok_rows, HD), jnp.float32),
    )
    key_all, value_all = (
        lax.all_gather(keys, "seq", axis=0, tiled=True),
        lax.all_gather(values, "seq", axis=0, tiled=True),
    )

    def forward_block(index, carry):
        kstart = index * block
        key_rows = lax.dynamic_slice_in_dim(key_all, kstart, block, 0)
        value_rows = lax.dynamic_slice_in_dim(value_all, kstart, block, 0)
        return forward_step(carry, key_rows, value_rows, kstart)

    top, lsum, acc = lax.fori_loop(0, live_blocks, forward_block, start_carry)
    heads_out = acc / lsum[..., None]
    attended = heads_out.transpose(2, 0, 1, 3).reshape(tok_rows, H * HD).astype(jnp.bfloat16)
    rowdot = jnp.sum(
        out_grad.astype(jnp.float32).reshape(tok_rows, KVH, GROUP, HD)
        * attended.astype(jnp.float32).reshape(tok_rows, KVH, GROUP, HD),
        axis=-1,
    ).transpose(1, 2, 0)

    def backward_block(index, carry):
        query_acc, partial_value = carry
        kstart = index * block
        key_rows = lax.dynamic_slice_in_dim(key_all, kstart, block, 0)
        value_rows = lax.dynamic_slice_in_dim(value_all, kstart, block, 0)
        visible = visible_of(kstart, block)
        scores = scores_of(key_rows, visible)
        probs = jnp.where(visible, jnp.exp(scores - top[..., None]) / lsum[..., None], 0.0)
        value_heads = value_rows.reshape(block, KVH, HD)
        key_heads = key_rows.reshape(block, KVH, HD)
        dprobs = jnp.einsum(
            "tkgd,skd->kgts", grad_heads, value_heads, preferred_element_type=jnp.float32
        )
        dscores = (probs * (dprobs - rowdot[..., None])).astype(jnp.bfloat16)
        query_acc = query_acc + jnp.einsum(
            "kgts,skd->kgtd", dscores, key_heads, preferred_element_type=jnp.float32
        )
        key_part = (
            jnp.einsum("kgts,tkgd->skd", dscores, qh, preferred_element_type=jnp.float32) * scale
        )
        value_part = jnp.einsum(
            "kgts,tkgd->skd",
            probs.astype(jnp.bfloat16),
            grad_heads,
            preferred_element_type=jnp.float32,
        )
        stacked = jnp.concatenate(
            [key_part.reshape(block, kv_width), value_part.reshape(block, kv_width)], axis=1
        )
        partial_value = lax.dynamic_update_slice(
            partial_value, stacked.astype(jnp.bfloat16), (kstart, 0)
        )
        return (query_acc, partial_value)

    back_carry = (
        jnp.zeros((KVH, GROUP, tok_rows, HD), jnp.float32),
        jnp.zeros((total_len, 2 * kv_width), jnp.bfloat16),
    )
    query_acc, partial_value = lax.fori_loop(0, live_blocks, backward_block, back_carry)
    summed = lax.psum_scatter(partial_value, "seq", scatter_dimension=0, tiled=True).astype(
        jnp.float32
    )
    query_grad = (
        (query_acc * scale).transpose(2, 0, 1, 3).reshape(tok_rows, H * HD).astype(jnp.bfloat16)
    )
    key_grad = summed[:, :kv_width].astype(jnp.bfloat16)
    value_grad = summed[:, kv_width:].astype(jnp.bfloat16)
    return (attended, query_grad, key_grad, value_grad)


def solution(mesh):
    in_specs = (
        P(("dp", "seq"), None),
        P(("dp", "seq"), None),
        P(("dp", "seq"), None),
        P("dp", None),
        P(("dp", "seq"), None),
    )
    out_specs = (
        P(("dp", "seq"), None),
        P(("dp", "seq"), None),
        P(("dp", "seq"), None),
        P(("dp", "seq"), None),
    )
    return jax.shard_map(shards, mesh=mesh, in_specs=in_specs, out_specs=out_specs, check_vma=False)
```

profile of v0, /device:TPU:42, one launch (start us, length us, event | category | flops | bytes accessed | tf_op | source)
XLA Modules:
  0.0 249.3 jit_solution(3896361902892705112)
XLA Ops:
  7.2 1.7 copy.56
  8.9 1.7 copy.58
  13.9 0.7 copy.55
  14.8 1.6 copy.62
  16.4 2.3 copy.57
  18.7 1.6 copy.59
  20.4 42.1 %all-gather.3.cloned.1.call-done = bf16[1024,512]{0,1:T(8,128)(2,1)} async-done(((bf16[128,512]{0,1:T(8,128)(2,1)}), bf16[1024,512]{0,1:T(8,128)(2,1)}) %all-gather.3.cloned.1.call-update) | async-done | bytes 1048592 | tf_op jit(solution)/shard_map/all_gather | solution.py:69
  62.5 53.0 %all-gather.5.cloned.1.call-done = bf16[1024,512]{0,1:T(8,128)(2,1)} async-done(((bf16[128,512]{0,1:T(8,128)(2,1)}), bf16[1024,512]{0,1:T(8,128)(2,1)}) %all-gather.5.cloned.1.call-update) | async-done | bytes 1048592 | tf_op jit(solution)/shard_map/all_gather | solution.py:70
  115.5 1.6 broadcast.53.clone
  117.1 10.0 %while.28 = (s32[]{:T(128)}, f32[4,8,128]{2,1,0:T(8,128)S(1)}, f32[4,8,128]{2,1,0:T(8,128)S(1)}, f32[4,8,128,128]{3,2,1,0:T(8,128)}, s32[]{:T(128)}, /*index=5*/...) while((s32[]{:T(128)}, f32[4,8,128]{2,1,0:T(8,128)S(1)}, ...), condition=%wide.region_6.7_spmd.clone, body=%wide.region_2.6_spmd.clone.sunk | while | flops 1102282880 | bytes 50868028 | solution.py:79
  117.4 1.3 constant_dynamic-slice_fusion.6
  118.7 1.5 fusion.69
  120.2 2.1 fusion.70
  122.3 3.4 %multiply_add_fusion.5 = f32[4,8,128,128]{3,2,1,0:T(8,128)S(1)} fusion(f32[4,8,128,128]{3,2,1,0:T(8,128)S(1)} %copy-done, bf16[512,4,128,1]{0,2,3,1:T(8,128)(2,1)S(1)} %bitcast.153, f32[4,512,128,8]{2,1,3,0:T(8,128)S(1)} %get-tuple-element.446, f32[4,8,128]{2,1,0:T(8,128)S(1)} %max.5, pred[128,512]{0,1:T(8,128)(4,1)S(1)} %compare_and_fusion.4, ...), kind=kOutput, calls=%fused_computation.9.clone.1 | convolution fusion | flops 548405248 | bytes 13205504 | tf_op jit(solution)/shard_map/while/body/kgts,skd->kgtd/dot_general | solution.py:55
  125.7 1.3 copy-done.1
  127.1 1.9 copy.60
  129.0 1.5 multiply_reduce_fusion
  130.5 1.6 broadcast.53
  132.1 1.6 broadcast_in_dim.53.clone
  133.7 17.2 %while.29 = (s32[]{:T(128)}, f32[4,8,128,128]{3,2,1,0:T(8,128)}, bf16[1024,1024]{1,0:T(8,128)(2,1)}, s32[]{:T(128)}, s32[16]{0:T(128)S(1)}, /*index=5*/s32[128]{...) while((s32[]{:T(128)}, f32[4,8,128,128]{3,2,1,0:T(8,128)}, ...), condition=%wide.region_10.11_spmd.clone, body=%wide.region_8.10_spmd.clone.sunk | while | flops 2706857984 | bytes 57339684 | solution.py:126
  134.0 1.3 constant_dynamic-slice_fusion.7
  135.3 3.8 %fusion.81 = f32[4,8,128,512]{2,3,1,0:T(8,128)S(1)} fusion(f32[4,8,128]{2,1,0:T(8,128)S(1)} %get-tuple-element.556, f32[4,8,128]{2,1,0:T(8,128)S(1)} %get-tuple-element.555, pred[128,512]{0,1:T(8,128)(4,1)S(1)} %compare_and_fusion.5, bf16[512,4,128,1]{0,2,3,1:T(8,128)(2,1)S(1)} %bitcast.149, bf16[128,4,8,128]{0,3,2,1:T(8,128)(2,1)} %get-tuple-element.554), kind=kOutput, calls=%fused_computation.28.clone.1 | convolution fusion | flops 547356672 | bytes 10059776 | tf_op jit(solution)/shard_map/while/body/tkgd,skd->kgts/dot_general | solution.py:37
  139.1 1.5 fusion.83
  140.6 1.4 fusion.82
  142.0 2.7 %fusion.84 = bf16[4,512,128]{1,2,0:T(8,128)(2,1)S(1)} fusion(bf16[4,8,128,512]{2,3,1,0:T(8,128)(2,1)S(1)} %fusion.82, bf16[128,4,8,128]{0,3,2,1:T(8,128)(2,1)} %get-tuple-element.554), kind=kOutput, calls=%fused_computation.36.clone.1 | convolution fusion | flops 537395200 | bytes 5767168 | tf_op jit(solution)/shard_map/while/body/kgts,tkgd->skd/dot_general | solution.py:106
  144.7 4.5 %convolution_add_fusion.2 = f32[4,8,128,128]{3,2,1,0:T(8,128)} fusion(f32[4,8,128,128]{3,2,1,0:T(8,128)} %get-tuple-element.530, bf16[4,8,128,512]{2,3,1,0:T(8,128)(2,1)S(1)} %fusion.82, bf16[512,4,128,1]{0,2,3,1:T(8,128)(2,1)S(1)} %bitcast.150), kind=kOutput, calls=%fused_computation.31.clone.1 | convolution fusion | flops 537395200 | bytes 8912896 | tf_op jit(solution)/shard_map/while/body/kgts,skd->kgtd/dot_general | solution.py:102
  149.9 1.1 constant_dynamic-update-slice_fusion.2
  150.9 2.3 copy.78
  153.2 1.9 fusion.31
  155.8 1.4 copy.93
  157.2 83.9 %reduce-scatter.2.cloned.1.call-done = bf16[128,1024]{1,0:T(8,128)(2,1)} async-done(((bf16[1024,1024]{1,0:T(8,128)(2,1)}), bf16[128,1024]{1,0:T(8,128)(2,1)}) %reduce-scatter.2.cloned.1.call-update) | async-done | bytes 262160 | tf_op jit(solution)/shard_map/reduce_scatter | solution.py:127
  241.1 1.7 fusion.32
  (30 shorter events, 2.9 us)
Async XLA Ops:
  7.2 55.3 %all-gather.3.cloned.1.call-start = ((), (), s32[]{:S(2)}) async-start(), calls=%async_computation.1 | async-start | bytes 1179648 | tf_op jit(solution)/shard_map/all_gather | solution.py:69
  8.9 106.6 %all-gather.5.cloned.1.call-start = ((), (), s32[]{:S(2)}) async-start(), calls=%async_computation.2 | async-start | bytes 1179648 | tf_op jit(solution)/shard_map/all_gather | solution.py:70
  10.6 230.4 %reduce-scatter.2.cloned.1.call-start = ((), (), s32[]{:S(2)}) async-start(), calls=%async_computation.3 | async-start | bytes 2359296 | tf_op jit(solution)/shard_map/reduce_scatter | solution.py:127
  120.1 2.2 copy-start
  125.7 1.4 copy-start.1
Sparse Core Ops, SparseCore 0:
  10.6 51.9 all-gather.2
  65.1 50.3 all-gather.4
  151.1 89.9 reduce-scatter.1
where the time goes:
time: 250 us; the launch traced here: 249 us
  waiting for transfers between devices  179 us (72%)
  local copies, waits for them, and re-layouts  28.3 us (11%)
  matrix products  18.8 us (8%)
  between operations  16.4 us (7%)
  other arithmetic  6.46 us (3%)
    reduce_scatter x1, waiting for transfers between devices, shards(): lax.psum_scatter(partial_value, 'seq', scatter_dimension=0, tiled=True)  83.9 us
    all_gather x1, waiting for transfers between devices, shards(): lax.all_gather(values, 'seq', axis=0, tiled=True)  53 us
    all_gather x1, waiting for transfers between devices, shards(): lax.all_gather(keys, 'seq', axis=0, tiled=True)  42.1 us
    unnamed x6, local copies, waits for them, and re-layouts  10.2 us
    dot_general x2, matrix products, scores_of(): jnp.einsum('tkgd,skd->kgts', qh, key_rows.reshape(-1, KVH, HD), preferred...  5.27 us
  transfers between devices with their start and end apart: 3, of which 3 were waited for; matrix products, arithmetic and copies ran while one was open for 6% of the time, Pallas kernels for 0%

commit v1 on v0

--- a/solution.py
+++ b/solution.py
@@ -67,7 +67,9 @@
     )
     key_all, value_all = (
         lax.all_gather(keys, "seq", axis=0, tiled=True),
-        lax.all_gather(values, "seq", axis=0, tiled=True),
+        jnp.concatenate(
+            lax.all_to_all(jnp.stack([values] * lax.axis_size("seq")), "seq", 0, 0), axis=0
+        ),
     )
 
     def forward_block(index, carry):

time: 250 us -> 198 us (0.79)
  the two profiles are of different devices: /device:TPU:42 before, /device:TPU:10 now
where the time goes in v1:
time: 198 us; the launch traced here: 197 us
  waiting for transfers between devices  114 us (58%)
  local copies, waits for them, and re-layouts  31.5 us (16%)
  matrix products  18.8 us (9%)
  between operations  16.7 us (8%)
  starting transfers between devices  9.28 us (5%)
  other arithmetic  6.46 us (3%)
    reduce_scatter x1, waiting for transfers between devices, shards(): lax.psum_scatter(partial_value, 'seq', scatter_dimension=0, tiled=True)  85.1 us
    all_gather x1, waiting for transfers between devices, shards(): lax.all_gather(keys, 'seq', axis=0, tiled=True)  26.8 us
    unnamed x9, local copies, waits for them, and re-layouts  11 us
    all_to_all x1, starting transfers between devices, shards(): lax.all_to_all(jnp.stack([values] * lax.axis_size('seq')), 'seq', 0, 0)  9.24 us
    dot_general x2, matrix products, scores_of(): jnp.einsum('tkgd,skd->kgts', qh, key_rows.reshape(-1, KVH, HD), preferred...  5.27 us
    dot_general x1, matrix products, backward_block(): jnp.einsum('kgts,skd->kgtd', dscores, key_heads, preferred_element_type=j...  4.52 us
  transfers between devices with their start and end apart: 3, of which 3 were waited for; matrix products, arithmetic and copies ran while one was open for 9% of the time, Pallas kernels for 0%

profile of v1, /device:TPU:10, one launch (start us, length us, event | category | flops | bytes accessed | tf_op | source)
XLA Modules:
  0.0 197.1 jit_solution(447239484237575102)
XLA Ops:
  7.2 1.7 copy.101
  10.0 1.1 stack.2
  11.1 9.2 %all-to-all-start = ((bf16[8,128,512]{1,2,0:T(8,128)(2,1)}), bf16[8,128,512]{1,2,0:T(8,128)(2,1)S(1)}, u32[]{:S(2)}, u32[]{:S(2)}) async-start(bf16[8,128,512]{1,2,0:T(8,128)(2,1)} %stack.2), calls=%async_computation | async-start | bytes 2097152 | tf_op jit(solution)/shard_map/all_to_all | solution.py:71
  25.1 2.3 %copy.102 = bf16[128,4096]{0,1:T(8,128)(2,1)} copy(bf16[128,4096]{1,0:T(8,128)(2,1)} %param.9) | data formatting | bytes 2097152 | tf_op args[0]
  27.4 1.6 copy.105
  29.1 2.3 %all-to-all-done = bf16[8,128,512]{1,2,0:T(8,128)(2,1)S(1)} async-done(((bf16[8,128,512]{1,2,0:T(8,128)(2,1)}), bf16[8,128,512]{1,2,0:T(8,128)(2,1)S(1)}, u32[]{:S(2)}, u32[]{:S(2)}) %all-to-all-start) | async-done | bytes 1048608 | tf_op jit(solution)/shard_map/all_to_all | solution.py:71
  31.4 1.3 copy.104
  32.7 2.3 %copy.106 = bf16[1024,512]{0,1:T(8,128)(2,1)} copy(bf16[1024,512]{1,0:T(8,128)(2,1)} %bitcast.156) | data formatting | bytes 2097152
  35.0 26.8 %all-gather.2.cloned.1.call-done = bf16[1024,512]{0,1:T(8,128)(2,1)} async-done(((bf16[128,512]{0,1:T(8,128)(2,1)}), bf16[1024,512]{0,1:T(8,128)(2,1)}) %all-gather.2.cloned.1.call-update) | async-done | bytes 1048592 | tf_op jit(solution)/shard_map/all_gather | solution.py:69
  61.8 1.6 broadcast.55.clone
  63.4 10.0 %while.28 = (s32[]{:T(128)}, f32[4,8,128]{2,1,0:T(8,128)S(1)}, f32[4,8,128]{2,1,0:T(8,128)S(1)}, f32[4,8,128,128]{3,2,1,0:T(8,128)}, s32[]{:T(128)}, /*index=5*/...) while((s32[]{:T(128)}, f32[4,8,128]{2,1,0:T(8,128)S(1)}, ...), condition=%wide.region_6.7_spmd.clone, body=%wide.region_2.6_spmd.clone.sunk | while | flops 1102282880 | bytes 50868028 | solution.py:81
  63.7 1.3 constant_dynamic-slice_fusion.6
  65.0 1.5 fusion.69
  66.5 2.1 %fusion.70 = f32[4,8,128]{2,1,0:T(8,128)S(1)} fusion(f32[4,512,128,8]{2,1,3,0:T(8,128)S(1)} %get-tuple-element.496, f32[4,8,128]{2,1,0:T(8,128)S(1)} %max.5, pred[128,512]{0,1:T(8,128)(4,1)S(1)} %compare_and_fusion.4), kind=kLoop, calls=%fused_computation.6.clone.1 | loop fusion | flops 10481664 | bytes 8486912 | tf_op jit(solution)/shard_map/while/body/reduce_sum | solution.py:54
  68.6 3.4 %multiply_add_fusion.5 = f32[4,8,128,128]{3,2,1,0:T(8,128)S(1)} fusion(f32[4,8,128,128]{3,2,1,0:T(8,128)S(1)} %copy-done, bf16[512,4,128,1]{0,2,3,1:T(8,128)(2,1)S(1)} %bitcast.154, f32[4,512,128,8]{2,1,3,0:T(8,128)S(1)} %get-tuple-element.496, f32[4,8,128]{2,1,0:T(8,128)S(1)} %max.5, pred[128,512]{0,1:T(8,128)(4,1)S(1)} %compare_and_fusion.4, ...), kind=kOutput, calls=%fused_computation.9.clone.1 | convolution fusion | flops 548405248 | bytes 13205504 | tf_op jit(solution)/shard_map/while/body/kgts,skd->kgtd/dot_general | solution.py:55
  72.0 1.3 copy-done.1
  73.4 1.9 copy.107
  75.3 1.5 multiply_reduce_fusion
  76.8 1.6 broadcast.55
  78.4 1.6 broadcast_in_dim.53.clone
  80.0 17.2 %while.29 = (s32[]{:T(128)}, f32[4,8,128,128]{3,2,1,0:T(8,128)}, bf16[1024,1024]{1,0:T(8,128)(2,1)}, s32[]{:T(128)}, s32[16]{0:T(128)S(1)}, /*index=5*/s32[128]{...) while((s32[]{:T(128)}, f32[4,8,128,128]{3,2,1,0:T(8,128)}, ...), condition=%wide.region_10.11_spmd.clone, body=%wide.region_8.10_spmd.clone.sunk | while | flops 2706857984 | bytes 57339684 | solution.py:128
  80.3 1.3 constant_dynamic-slice_fusion.7
  81.6 3.8 %fusion.81 = f32[4,8,128,512]{2,3,1,0:T(8,128)S(1)} fusion(f32[4,8,128]{2,1,0:T(8,128)S(1)} %get-tuple-element.606, f32[4,8,128]{2,1,0:T(8,128)S(1)} %get-tuple-element.605, pred[128,512]{0,1:T(8,128)(4,1)S(1)} %compare_and_fusion.5, bf16[512,4,128,1]{0,2,3,1:T(8,128)(2,1)S(1)} %bitcast.150, bf16[128,4,8,128]{0,3,2,1:T(8,128)(2,1)} %get-tuple-element.604), kind=kOutput, calls=%fused_computation.28.clone.1 | convolution fusion | flops 547356672 | bytes 10059776 | tf_op jit(solution)/shard_map/while/body/tkgd,skd->kgts/dot_general | solution.py:37
  85.4 1.5 fusion.83
  86.9 1.4 fusion.82
  88.3 2.7 %fusion.84 = bf16[4,512,128]{1,2,0:T(8,128)(2,1)S(1)} fusion(bf16[4,8,128,512]{2,3,1,0:T(8,128)(2,1)S(1)} %fusion.82, bf16[128,4,8,128]{0,3,2,1:T(8,128)(2,1)} %get-tuple-element.604), kind=kOutput, calls=%fused_computation.36.clone.1 | convolution fusion | flops 537395200 | bytes 5767168 | tf_op jit(solution)/shard_map/while/body/kgts,tkgd->skd/dot_general | solution.py:108
  91.0 4.5 %convolution_add_fusion.2 = f32[4,8,128,128]{3,2,1,0:T(8,128)} fusion(f32[4,8,128,128]{3,2,1,0:T(8,128)} %get-tuple-element.580, bf16[4,8,128,512]{2,3,1,0:T(8,128)(2,1)S(1)} %fusion.82, bf16[512,4,128,1]{0,2,3,1:T(8,128)(2,1)S(1)} %bitcast.151), kind=kOutput, calls=%fused_computation.31.clone.1 | convolution fusion | flops 537395200 | bytes 8912896 | tf_op jit(solution)/shard_map/while/body/kgts,skd->kgtd/dot_general | solution.py:104
  97.2 2.3 %copy.126 = bf16[128,4096]{1,0:T(8,128)(2,1)} copy(bf16[128,4096]{0,1:T(8,128)(2,1)} %bitcast.158) | data formatting | bytes 2097152 | tf_op jit(solution)/shard_map/convert_element_type | solution.py:83
  99.5 1.9 fusion.31
  102.1 1.4 copy.141
  103.5 85.1 %reduce-scatter.2.cloned.1.call-done = bf16[128,1024]{1,0:T(8,128)(2,1)} async-done(((bf16[1024,1024]{1,0:T(8,128)(2,1)}), bf16[128,1024]{1,0:T(8,128)(2,1)}) %reduce-scatter.2.cloned.1.call-update) | async-done | bytes 262160 | tf_op jit(solution)/shard_map/reduce_scatter | solution.py:129
  188.6 1.7 fusion.32
  (34 shorter events, 6.3 us)
Async XLA Ops:
  7.2 17.3 %copy-start.2 = (bf16[128,4096]{1,0:T(8,128)(2,1)S(1)}, bf16[128,4096]{1,0:T(8,128)(2,1)}, u32[]{:S(2)}) copy-start(bf16[128,4096]{1,0:T(8,128)(2,1)} %param.13) | copy-start | bytes 3145732
  7.2 54.6 %all-gather.2.cloned.1.call-start = ((), (), s32[]{:S(2)}) async-start(), calls=%async_computation.2 | async-start | bytes 1179648 | tf_op jit(solution)/shard_map/all_gather | solution.py:69
  11.1 20.2 %all-to-all-start = ((bf16[8,128,512]{1,2,0:T(8,128)(2,1)}), bf16[8,128,512]{1,2,0:T(8,128)(2,1)S(1)}, u32[]{:S(2)}, u32[]{:S(2)}) async-start(bf16[8,128,512]{1,2,0:T(8,128)(2,1)} %stack.2), calls=%async_computation | async-start | bytes 2097152 | tf_op jit(solution)/shard_map/all_to_all | solution.py:71
  20.4 168.2 %reduce-scatter.2.cloned.1.call-start = ((), (), s32[]{:S(2)}) async-start(), calls=%async_computation.3 | async-start | bytes 2359296 | tf_op jit(solution)/shard_map/reduce_scatter | solution.py:129
  66.4 2.2 %copy-start = (f32[4,8,128,128]{3,2,1,0:T(8,128)S(1)}, f32[4,8,128,128]{3,2,1,0:T(8,128)}, u32[]{:S(2)}) copy-start(f32[4,8,128,128]{3,2,1,0:T(8,128)} %get-tuple-element.534) | copy-start | bytes 6291460 | tf_op jit(solution)/shard_map/while
  72.0 1.4 copy-start.1
Sparse Core Ops, SparseCore 0:
  10.6 51.1 all-gather.1
  97.4 91.1 reduce-scatter.1
